TPU v7x, 32 devices: a whole 2x2x4 slice. The times are simulated.
32 devices in a mesh: tm: 4 (over x, core), freq: 8 (over z, y).
Axes of the slice: x: 2, y: 2, z: 4, core: 2. Of those that a mesh axis runs over, the one named last changes fastest.
Arguments:
- visibilities: float32 [2, 4, 32, 8, 2016], P(None, None, 'tm', 'freq'), may hold values from -48 to 48
- sky_model: float32 [2, 4, 32, 8, 2016], P(None, None, 'tm', 'freq'), may hold values from -3 to 3
- gain_time: float32 [2, 2, 8, 64], P(None, None, 'tm'), may hold values from -4 to 4
- gain_band: float32 [2, 2, 8, 64], P(None, None, 'freq'), may hold values from -2.5 to 2.5
- delay_start: float32 [2, 64], replicated, may hold values from -2.2 to 2.2
- first_antenna: int32 [2016], replicated, may hold values from 0 to 63, as said below
- second_antenna: int32 [2016], replicated, may hold values from 0 to 63
Outputs:
- solved_time: float32 [2, 2, 8, 64], P(None, None, 'tm')
- solved_band: float32 [2, 2, 8, 64], P(None, None, 'freq')
- solved_delay: float32 [2, 64], replicated
- weights: float32 [32, 2016], P('tm')
- residual: float32 [2, 4, 32, 8, 2016], P(None, None, 'tm', 'freq')
Inputs may be any that keep to these rules, and one draw needn't show every extreme that they name: first_antenna and second_antenna together name every unordered pair of distinct antennas of the 64 exactly once, in an order and orientation drawn from the seed.
All inputs are finite; a program needn't handle non-finite values.
Results may differ from a plain program's by a relative error of at most 0.00013.
Values sent between devices are 32-bit elements; how exact they have to be, the bound alone decides.
A program may use at most 64 MiB of HBM per device.

v0:
```python
import functools
import math

import jax
import jax.numpy as jnp
from jax import lax
from jax.experimental import pallas as pl
from jax.experimental.pallas import tpu as pltpu
from jax.sharding import PartitionSpec as P

INTERVAL_TIMES = 4
SWEEPS = 2
FULL_TURN = 2.0 * math.pi
DAMPING = 0.5
EPSILON = 1e-06
LANES = 128
POLS = 2
UNROLLED_PEERS = 8


def cmul(a, b):
    return (a[0] * b[0] - a[1] * b[1], a[0] * b[1] + a[1] * b[0])


def conj_mul(a, b):
    return (a[0] * b[0] + a[1] * b[1], a[0] * b[1] - a[1] * b[0])


def power(a):
    return a[0] * a[0] + a[1] * a[1]


def split3(x):
    high = x.astype(jnp.bfloat16)
    rest = x - high.astype(jnp.float32)
    middle = rest.astype(jnp.bfloat16)
    low = (rest - middle.astype(jnp.float32)).astype(jnp.bfloat16)
    return high, middle, low


def each_peer(count, action):
    if count <= UNROLLED_PEERS:
        for step in range(1, count):
            action(step)
    else:
        lax.fori_loop(1, count, lambda step, carry: (action(step), carry)[1], 0)


def maybe(condition, action):
    if condition is True:
        action()
    else:
        pl.when(condition)(action)


def kernel(
    sizes,
    vis,
    sky,
    params,
    first,
    second,
    out_params,
    out_weights,
    out_residual,
    hot,
    u_ref,
    q_ref,
    wide,
    terms,
    s_ref,
    rs_ref,
    w_ref,
    time_ref,
    band_ref,
    turn_tm_ref,
    turn_ref,
    rs_sem,
    ag_sem,
    time_sem,
    band_sem,
    turn_tm_sem,
    turn_sem,
):
    n_freq, n_tm, channels, times, baselines, chunks, width = sizes
    intervals = times // INTERVAL_TIMES
    ants = LANES // POLS
    padded = chunks * width
    f_me = lax.axis_index("freq")
    t_me = lax.axis_index("tm")

    barrier = pltpu.get_barrier_semaphore()

    def greet(axis, count, me):
        def one(step):
            pl.semaphore_signal(
                barrier,
                inc=1,
                device_id={axis: lax.rem(me + step, count)},
                device_id_type=pl.DeviceIdType.MESH,
            )

        each_peer(count, one)

    greet("freq", n_freq, f_me)
    greet("tm", n_tm, t_me)

    def remote(src, dst, sem, step, axis, count, me):
        return pltpu.make_async_remote_copy(
            src_ref=src,
            dst_ref=dst,
            send_sem=sem.at[0, step],
            recv_sem=sem.at[1, step],
            device_id={axis: lax.rem(me + step, count)},
            device_id_type=pl.DeviceIdType.MESH,
        )

    def exchange(buf, tile, sem, axis, count, me):
        buf[me] = tile

        def copy(step):
            return remote(buf.at[me], buf.at[me], sem, step, axis, count, me)

        each_peer(count, lambda step: copy(step).start())
        each_peer(count, lambda step: copy(step).wait_recv())
        total = jnp.sum(buf[...], axis=0)
        each_peer(count, lambda step: copy(step).wait_send())
        return total

    row_ant = lax.rem(lax.broadcasted_iota(jnp.int32, (LANES, baselines), 0), ants)
    hot[:, padded - LANES : padded] = jnp.zeros((LANES, LANES), jnp.bfloat16)
    hot[:, 2 * padded - LANES : 2 * padded] = jnp.zeros((LANES, LANES), jnp.bfloat16)
    hot[:, 0:baselines] = (row_ant == first[...]).astype(jnp.float32).astype(jnp.bfloat16)
    hot[:, padded : padded + baselines] = (
        (row_ant == second[...]).astype(jnp.float32).astype(jnp.bfloat16)
    )

    lane = lax.broadcasted_iota(jnp.int32, (times, LANES), 1)
    row = lax.broadcasted_iota(jnp.int32, (times, LANES), 0)
    lower = lane < ants
    number = jnp.broadcast_to(f_me, (times, LANES)).astype(jnp.float32)
    frequency = (number + 0.5) / channels - 0.5
    turning = FULL_TURN * frequency

    def spread(rows):
        value = jnp.zeros((times, LANES), jnp.float32)
        for i in range(intervals):
            value = jnp.where(row // INTERVAL_TIMES == i, rows[i], value)
        return value

    def stack_rows(rows, height):
        index = lax.broadcasted_iota(jnp.int32, (height, LANES), 0)
        value = jnp.zeros((height, LANES), jnp.float32)
        for i, one in enumerate(rows):
            value = jnp.where(index == i, one, value)
        return value

    def row_of(i):
        return params[i : i + 1, :]

    g_time = tuple(
        spread([row_of(part * intervals + i) for i in range(intervals)]) for part in range(2)
    )
    base = 2 * intervals
    full = (times, LANES)
    g_band = tuple(jnp.broadcast_to(row_of(base + part), full) for part in range(2))
    turns = jnp.broadcast_to(row_of(base + 2), full)

    def chunk(c):
        return slice(c * width, (c + 1) * width)

    def load(ref, c):
        return [
            [(ref[2 * a + b, :, chunk(c)], ref[4 + 2 * a + b, :, chunk(c)]) for b in range(2)]
            for a in range(2)
        ]

    for c in range(chunks):
        v, k = load(vis, c), load(sky, c)
        for a in range(2):
            for b in range(2):
                u = conj_mul(k[a][b], v[a][b])
                u_ref[2 * a + b, :, chunk(c)] = u[0]
                u_ref[4 + 2 * a + b, :, chunk(c)] = u[1]
                q_ref[2 * a + b, :, chunk(c)] = power(k[a][b])

    def chain():
        angle = FULL_TURN * turns * frequency
        phasor = (jnp.cos(angle), jnp.sin(angle))
        band_delay = cmul(g_band, phasor)
        return cmul(g_time, band_delay), band_delay, phasor

    def antenna_rows(g):
        zero = jnp.zeros(full, jnp.float32)
        rows = []
        for part in range(2):
            rows.append(jnp.where(lower, g[part], zero))
            rows.append(jnp.where(lower, zero, g[part]))
        return jnp.concatenate(split3(jnp.concatenate(rows, axis=0)), axis=0)

    def gathered(rows, c, offset):
        got = jnp.dot(
            rows,
            hot[:, offset + c * width : offset + (c + 1) * width],
            preferred_element_type=jnp.float32,
        )
        size = 4 * times
        got = got[0:size] + got[size : 2 * size] + got[2 * size : 3 * size]
        part = [got[i * times : (i + 1) * times] for i in range(4)]
        return [(part[0], part[2]), (part[1], part[3])]

    def both(rows, c):
        return gathered(rows, c, 0), gathered(rows, c, padded)

    def residual_of(c, gp, gq):
        v, k = load(vis, c), load(sky, c)
        result = [[None, None], [None, None]]
        for a in range(2):
            for b in range(2):
                m = conj_mul(gq[b], cmul(gp[a], k[a][b]))
                result[a][b] = (v[a][b][0] - m[0], v[a][b][1] - m[1])
        return result

    def products(c, gp, gq):
        u = load(u_ref, c)
        q = [[q_ref[2 * a + b, :, chunk(c)] for b in range(2)] for a in range(2)]
        pp, pq = [power(x) for x in gp], [power(x) for x in gq]
        lead = [[None] * 2, [None] * 2]
        trail = [[None] * 2, [None] * 2]
        for i in range(2):
            x, y = cmul(u[i][0], gq[0]), cmul(u[i][1], gq[1])
            lead[0][i], lead[1][i] = x[0] + y[0], x[1] + y[1]
            x, y = conj_mul(u[0][i], gp[0]), conj_mul(u[1][i], gp[1])
            trail[0][i], trail[1][i] = x[0] + y[0], x[1] + y[1]
        lead_power = [q[i][0] * pq[0] + q[i][1] * pq[1] for i in range(2)]
        trail_power = [q[0][i] * pp[0] + q[1][i] * pp[1] for i in range(2)]
        return lead[0] + lead[1] + lead_power, trail[0] + trail[1] + trail_power

    def put_terms(c, tiles, offset, weight):
        stacked = jnp.concatenate([weight * tile for tile in tiles], axis=0)
        size = 6 * times
        for i, part in enumerate(split3(stacked)):
            terms[i * size : (i + 1) * size, offset + c * width : offset + (c + 1) * width] = part

    def antenna_sums():
        got = lax.dot_general(
            terms[...],
            hot[...],
            (((1,), (1,)), ((), ())),
            preferred_element_type=jnp.float32,
        )
        size = 6 * times
        got = got[0:size] + got[size : 2 * size] + got[2 * size : 3 * size]
        part = [got[i * times : (i + 1) * times] for i in range(6)]
        return [jnp.where(lower, part[2 * i], part[2 * i + 1]) for i in range(3)]

    def normal(g, weights_at):
        rows = antenna_rows(g)
        for c in range(chunks):
            gp, gq = both(rows, c)
            lead, trail = products(c, gp, gq)
            put_terms(c, lead, 0, weights_at(c))
            put_terms(c, trail, padded, weights_at(c))
        return finish_normal(g)

    def finish_normal(g):
        real, imag, e = antenna_sums()
        return (real - g[0] * e, imag - g[1] * e), e

    def over_times(x):
        return jnp.sum(x, axis=0, keepdims=True)

    owners = chunks
    all_own = owners == n_freq

    def owns(index):
        return True if all_own else index < owners

    for sweep in range(SWEEPS):
        g, band_delay, phasor = chain()
        rows = antenna_rows(g)
        kept = []
        for c in range(chunks):
            gp, gq = both(rows, c)
            r = residual_of(c, gp, gq)
            s_ref[sweep, c] = power(r[0][0]) + power(r[0][1]) + power(r[1][0]) + power(r[1][1])
            kept.append((gp, gq))
        if sweep == 0:
            pl.semaphore_wait(barrier, n_freq - 1 + n_tm - 1)

        def scatter_copy(step):
            peer = lax.rem(f_me + step, n_freq)
            return remote(
                s_ref.at[sweep, peer],
                rs_ref.at[sweep, step],
                rs_sem.at[sweep],
                step,
                "freq",
                n_freq,
                f_me,
            )

        def send_part(step):
            peer = lax.rem(f_me + step, n_freq)
            maybe(owns(peer), lambda: scatter_copy(step).start())

        each_peer(n_freq, send_part)

        for c in range(chunks):
            gp, gq = kept[c]
            lead, trail = products(c, gp, gq)
            for i, tile in enumerate(lead + trail):
                wide[i, :, chunk(c)] = tile

        def own_copy(step):
            return remote(
                w_ref.at[sweep, f_me],
                w_ref.at[sweep, f_me],
                ag_sem.at[sweep],
                step,
                "freq",
                n_freq,
                f_me,
            )

        def reduce_own():
            def arrive(step):
                pltpu.make_async_copy(
                    rs_ref.at[sweep, step], rs_ref.at[sweep, step], rs_sem.at[sweep, 1, step]
                ).wait()

            each_peer(n_freq, arrive)
            total = s_ref[sweep, f_me] + jnp.sum(rs_ref[sweep, 1:n_freq], axis=0)
            w_ref[sweep, f_me] = 1.0 / (total / (4 * channels) + EPSILON)
            each_peer(n_freq, lambda step: own_copy(step).start())

        maybe(owns(f_me), reduce_own)

        def receive_weights(step):
            origin = lax.rem(f_me + n_freq - step, n_freq)

            def arrive():
                pltpu.make_async_copy(
                    w_ref.at[sweep, 0], w_ref.at[sweep, 0], ag_sem.at[sweep, 1, step]
                ).wait()

            maybe(owns(origin), arrive)

        each_peer(n_freq, receive_weights)

        def sent(step):
            peer = lax.rem(f_me + step, n_freq)
            maybe(owns(peer), lambda: scatter_copy(step).wait_send())
            maybe(owns(f_me), lambda: own_copy(step).wait_send())

        each_peer(n_freq, sent)

        for c in range(chunks):
            tiles = [wide[i, :, chunk(c)] for i in range(12)]
            put_terms(c, tiles[:6], 0, w_ref[sweep, c])
            put_terms(c, tiles[6:], padded, w_ref[sweep, c])
        a, e = finish_normal(g)
        n = conj_mul(band_delay, a)
        d = power(band_delay) * e
        rows_out = []
        for value in (n[0], n[1], d):
            for i in range(intervals):
                span = slice(i * INTERVAL_TIMES, (i + 1) * INTERVAL_TIMES)
                rows_out.append(over_times(value[span]))
        tile = stack_rows(rows_out, time_ref.shape[2])
        total = exchange(time_ref.at[sweep], tile, time_sem.at[sweep], "freq", n_freq, f_me)
        part = [total[i : i + 1] for i in range(3 * intervals)]
        g_time = tuple(
            g_time[p]
            + spread(
                [
                    DAMPING * part[p * intervals + i] / part[2 * intervals + i]
                    for i in range(intervals)
                ]
            )
            for p in range(2)
        )

        g, band_delay, phasor = chain()
        a, e = normal(g, lambda c: w_ref[sweep, c])
        other = cmul(g_time, phasor)
        n = conj_mul(other, a)
        tile = stack_rows([over_times(x) for x in (n[0], n[1], power(other) * e)], 8)
        total = exchange(band_ref.at[sweep], tile, band_sem.at[sweep], "tm", n_tm, t_me)
        g_band = tuple(
            g_band[p] + jnp.broadcast_to(DAMPING * total[p : p + 1] / total[2:3], full)
            for p in range(2)
        )

        g, band_delay, phasor = chain()
        a, e = normal(g, lambda c: w_ref[sweep, c])
        n = turning * conj_mul(g, a)[1]
        d = turning * turning * power(g) * e
        tile = stack_rows([over_times(n), over_times(d)], 8)
        tile = exchange(turn_tm_ref.at[sweep], tile, turn_tm_sem.at[sweep], "tm", n_tm, t_me)
        total = exchange(turn_ref.at[sweep], tile, turn_sem.at[sweep], "freq", n_freq, f_me)
        turns = turns + jnp.broadcast_to(DAMPING * total[0:1] / total[1:2], full)

    g, band_delay, phasor = chain()
    rows = antenna_rows(g)
    for c in range(chunks):
        gp, gq = both(rows, c)
        r = residual_of(c, gp, gq)
        stop = min(baselines, (c + 1) * width)
        here = slice(c * width, stop)
        size = stop - c * width
        for i in range(2):
            for a in range(2):
                for b in range(2):
                    out_residual[4 * i + 2 * a + b, :, here] = r[a][b][i][:, :size]
        out_weights[:, here] = w_ref[SWEEPS - 1, c][:, :size]
    rows_out = [
        g_time[p][i * INTERVAL_TIMES : i * INTERVAL_TIMES + 1]
        for p in range(2)
        for i in range(intervals)
    ]
    rows_out += [g_band[0][0:1], g_band[1][0:1], turns[0:1]]
    out_params[...] = stack_rows(rows_out, out_params.shape[0])


def ceil_to(value, step):
    return -(-value // step) * step


def shards(n_freq, n_tm, vis, sky, gain_time, gain_band, delay_start, first, second):
    times, local_channels, baselines = vis.shape[2:]
    antennas = gain_time.shape[-1]
    assert local_channels == 1 and POLS * antennas == LANES
    intervals = times // INTERVAL_TIMES
    channels = local_channels * n_freq
    tiles = -(-baselines // LANES)
    chunks = max(c for c in range(1, min(n_freq, tiles) + 1) if tiles % c == 0)
    width = tiles * LANES // chunks
    padded = tiles * LANES
    margin = ((0, 0), (0, 0), (0, padded - baselines))
    flat = (8, times, baselines)
    count = 2 * intervals + 3
    height = ceil_to(count, 8)
    params = jnp.concatenate(
        [
            gain_time.transpose(0, 2, 1, 3).reshape(2 * intervals, LANES),
            gain_band.transpose(0, 2, 1, 3).reshape(2, LANES),
            delay_start.reshape(1, LANES),
            jnp.zeros((height - count, LANES), jnp.float32),
        ],
        axis=0,
    )
    sizes = (n_freq, n_tm, channels, times, baselines, chunks, width)
    f32 = jnp.float32
    vmem = pl.BlockSpec(memory_space=pltpu.VMEM)
    sems = [
        pltpu.SemaphoreType.DMA((SWEEPS, 2, count))
        for count in (n_freq, n_freq, n_freq, n_tm, n_tm, n_freq)
    ]
    solved, weights, residual = pl.pallas_call(
        functools.partial(kernel, sizes),
        out_shape=(
            jax.ShapeDtypeStruct((height, LANES), f32),
            jax.ShapeDtypeStruct((times, baselines), f32),
            jax.ShapeDtypeStruct(flat, f32),
        ),
        in_specs=[vmem] * 5,
        out_specs=(vmem,) * 3,
        scratch_shapes=[
            pltpu.VMEM((LANES, 2 * padded), jnp.bfloat16),
            pltpu.VMEM((8, times, padded), f32),
            pltpu.VMEM((4, times, padded), f32),
            pltpu.VMEM((12, times, padded), f32),
            pltpu.VMEM((18 * times, 2 * padded), jnp.bfloat16),
            pltpu.VMEM((SWEEPS, chunks, times, width), f32),
            pltpu.VMEM((SWEEPS, n_freq, times, width), f32),
            pltpu.VMEM((SWEEPS, chunks, times, width), f32),
            pltpu.VMEM((SWEEPS, n_freq, ceil_to(3 * intervals, 8), LANES), f32),
            pltpu.VMEM((SWEEPS, n_tm, 8, LANES), f32),
            pltpu.VMEM((SWEEPS, n_tm, 8, LANES), f32),
            pltpu.VMEM((SWEEPS, n_freq, 8, LANES), f32),
            *sems,
        ],
        compiler_params=pltpu.CompilerParams(collective_id=0, has_side_effects=True),
    )(
        jnp.pad(vis.reshape(flat), margin),
        jnp.pad(sky.reshape(flat), margin),
        params,
        first.reshape(1, baselines),
        second.reshape(1, baselines),
    )
    base = 2 * intervals
    solved_time = solved[0:base].reshape(2, intervals, POLS, antennas).transpose(0, 2, 1, 3)
    solved_band = solved[base : base + 2].reshape(2, 1, POLS, antennas).transpose(0, 2, 1, 3)
    solved_delay = solved[base + 2].reshape(POLS, antennas)
    return solved_time, solved_band, solved_delay, weights, residual.reshape(vis.shape)


def solution(mesh):
    in_specs = (
        P(None, None, "tm", "freq", None),
        P(None, None, "tm", "freq", None),
        P(None, None, "tm", None),
        P(None, None, "freq", None),
        P(),
        P(),
        P(),
    )
    out_specs = (
        P(None, None, "tm", None),
        P(None, None, "freq", None),
        P(),
        P("tm", None),
        P(None, None, "tm", "freq", None),
    )
    body = functools.partial(shards, mesh.shape["freq"], mesh.shape["tm"])
    return jax.shard_map(body, mesh=mesh, in_specs=in_specs, out_specs=out_specs, check_vma=False)
```

profile of v0, /device:TPU:0, one launch (start us, length us, event | category | flops | bytes accessed | tf_op | source)
XLA Modules:
  0.0 72.6 jit_solution(10809001699625191924)
XLA Ops:
  0.6 0.7 copy-done.5
  1.3 0.1 reshape.37
  1.4 0.1 pad.12.clone
  1.5 0.5 broadcast.12
  2.0 0.1 copy-done.4
  2.1 0.7 reduce.7
  2.8 0.1 reshape_transpose.3
  2.8 0.0 copy-done.2
  2.8 0.1 reshape.36
  2.9 0.7 maximum_maximum_fusion.params
  3.6 1.2 %copy.16 = f32[2,4,8,1,2016]{4,2,3,1,0:T(8,128)S(1)} copy(f32[2,4,8,1,2016]{4,3,2,1,0:T(1,128)} %param.7) | data formatting | bytes 1032192
  4.8 0.0 copy-start
  4.8 0.8 %pad.7.vis = f32[8,8,2048]{2,1,0:T(8,128)} pad(f32[8,8,2016]{2,1,0:T(8,128)S(1)} %bitcast.12, f32[]{:T(128)} %constant.1.clone.1), padding=0_0x0_0x0_32 | pad | bytes 1040388 | tf_op jit(solution)/shard_map/jit(_pad)/pad | solution.py:486
  5.6 0.4 copy-done
  6.0 0.2 copy.17
  6.2 0.8 %pad.8.sky = f32[8,8,2048]{2,1,0:T(8,128)} pad(f32[8,8,2016]{2,1,0:T(8,128)S(1)} %bitcast.11, f32[]{:T(128)} %constant.1.clone.1), padding=0_0x0_0x0_32 | pad | bytes 1040388 | tf_op jit(solution)/shard_map/jit(_pad)/pad | solution.py:487
  7.0 60.5 %shard_map.110 = (f32[8,128]{1,0:T(8,128)}, f32[8,2016]{1,0:T(8,128)}, f32[8,8,2016]{2,1,0:T(8,128)}) custom-call(f32[8,8,2048]{2,1,0:T(8,128)} %pad.7.vis, f32[8,8,2048]{2,1,0:T(8,128)} %pad.8.sky, f32[8,128]{1,0:T(8,128)} %maximum_maximum_fusion.params, s32[1,2016]{1,0:T(1,128)} %bitcast.14, s32[1,2016]{1,0:T(1,128)} %bitcast.15), custom_call_target="tpu_custom_call" | custom-call | tf_op jit(solution)/shard_map/pallas_call | solution.py:460
  67.6 2.4 %copy.15 = f32[2,4,8,1,2016]{4,3,2,1,0:T(1,128)} copy(f32[2,4,8,1,2016]{4,2,1,0,3:T(8,128)} %bitcast.13) | data formatting | bytes 1032192
  70.0 0.6 reshape_squeeze.3
  70.6 0.7 transpose_reshape.3
  71.3 0.1 reshape.40
  71.4 0.6 copy.19
  72.0 0.0 copy-done.1
  72.0 0.6 copy.21
  (10 shorter events, 0.0 us)
Async XLA Ops:
  0.6 0.7 copy-start.5
  1.4 0.7 copy-start.4
  2.1 0.8 %copy-start.2 = (f32[2,2,2,64]{3,2,1,0:T(2,128)S(1)}, f32[2,2,2,64]{3,2,1,0:T(2,128)}, u32[]{:S(2)}) copy-start(f32[2,2,2,64]{3,2,1,0:T(2,128)} %param.9) | copy-start | bytes 6148
  4.8 1.2 %copy-start = (f32[2,4,8,1,2016]{4,3,2,1,0:T(1,128)S(1)}, f32[2,4,8,1,2016]{4,3,2,1,0:T(1,128)}, u32[]{:S(2)}) copy-start(f32[2,4,8,1,2016]{4,3,2,1,0:T(1,128)} %param.8) | copy-start | bytes 1548292
  67.5 2.4 %copy-start.3 = (f32[8,128]{1,0:T(8,128)S(1)}, f32[8,128]{1,0:T(8,128)}, u32[]{:S(2)}) copy-start(f32[8,128]{1,0:T(8,128)} %get-tuple-element.8) | copy-start | bytes 12292
  67.6 4.4 %copy-start.1 = (f32[8,2016]{1,0:T(8,128)S(1)}, f32[8,2016]{1,0:T(8,128)}, u32[]{:S(2)}) copy-start(f32[8,2016]{1,0:T(8,128)} %get-tuple-element.24) | copy-start | bytes 193540
where the time goes:
time: 73 us; the launch traced here: 72.6 us
  Pallas kernels  60.5 us (83%)
  local copies, waits for them, and re-layouts  10.1 us (14%)
  other arithmetic  1.34 us (2%)
    pallas_call x1, Pallas kernels, shards(): pl.pallas_call(functools.partial(kernel, sizes), out_shape=(jax.ShapeDtyp...  60.5 us
    unnamed x17, local copies, waits for them, and re-layouts  6.08 us

commit v1 on v0

--- a/solution.py
+++ b/solution.py
@@ -55,14 +55,18 @@
 
 def kernel(
     sizes,
-    vis,
-    sky,
-    params,
+    vis_raw,
+    sky_raw,
+    gain_time,
+    gain_band,
+    delay_start,
     first,
     second,
     out_params,
     out_weights,
     out_residual,
+    vis,
+    sky,
     hot,
     u_ref,
     q_ref,
@@ -73,13 +77,11 @@
     w_ref,
     time_ref,
     band_ref,
-    turn_tm_ref,
     turn_ref,
     rs_sem,
     ag_sem,
     time_sem,
     band_sem,
-    turn_tm_sem,
     turn_sem,
 ):
     n_freq, n_tm, channels, times, baselines, chunks, width = sizes
@@ -91,19 +93,24 @@
 
     barrier = pltpu.get_barrier_semaphore()
 
-    def greet(axis, count, me):
-        def one(step):
-            pl.semaphore_signal(
-                barrier,
-                inc=1,
-                device_id={axis: lax.rem(me + step, count)},
-                device_id_type=pl.DeviceIdType.MESH,
-            )
-
-        each_peer(count, one)
-
-    greet("freq", n_freq, f_me)
-    greet("tm", n_tm, t_me)
+    def each_other(action):
+        for across in range(n_tm):
+            if across:
+                action(across, 0)
+            each_peer(n_freq, lambda step: action(across, step))
+
+    def device_at(across, step):
+        return {"tm": lax.rem(t_me + across, n_tm), "freq": lax.rem(f_me + step, n_freq)}
+
+    def greet(across, step):
+        pl.semaphore_signal(
+            barrier,
+            inc=1,
+            device_id=device_at(across, step),
+            device_id_type=pl.DeviceIdType.MESH,
+        )
+
+    each_other(greet)
 
     def remote(src, dst, sem, step, axis, count, me):
         return pltpu.make_async_remote_copy(
@@ -127,6 +134,25 @@
         each_peer(count, lambda step: copy(step).wait_send())
         return total
 
+    def exchange_all(buf, tile, sem):
+        buf[t_me, f_me] = tile
+
+        def copy(across, step):
+            return pltpu.make_async_remote_copy(
+                src_ref=buf.at[t_me, f_me],
+                dst_ref=buf.at[t_me, f_me],
+                send_sem=sem.at[0, across, step],
+                recv_sem=sem.at[1, across, step],
+                device_id=device_at(across, step),
+                device_id_type=pl.DeviceIdType.MESH,
+            )
+
+        each_other(lambda across, step: copy(across, step).start())
+        each_other(lambda across, step: copy(across, step).wait_recv())
+        total = jnp.sum(jnp.sum(buf[...], axis=0), axis=0)
+        each_other(lambda across, step: copy(across, step).wait_send())
+        return total
+
     row_ant = lax.rem(lax.broadcasted_iota(jnp.int32, (LANES, baselines), 0), ants)
     hot[:, padded - LANES : padded] = jnp.zeros((LANES, LANES), jnp.bfloat16)
     hot[:, 2 * padded - LANES : 2 * padded] = jnp.zeros((LANES, LANES), jnp.bfloat16)
@@ -155,16 +181,24 @@
             value = jnp.where(index == i, one, value)
         return value
 
-    def row_of(i):
-        return params[i : i + 1, :]
-
+    def packed(halves):
+        return jnp.concatenate(halves, axis=1)
+
+    full = (times, LANES)
     g_time = tuple(
-        spread([row_of(part * intervals + i) for i in range(intervals)]) for part in range(2)
+        spread(
+            [
+                packed([gain_time[part, p, i : i + 1, :] for p in range(POLS)])
+                for i in range(intervals)
+            ]
+        )
+        for part in range(2)
     )
-    base = 2 * intervals
-    full = (times, LANES)
-    g_band = tuple(jnp.broadcast_to(row_of(base + part), full) for part in range(2))
-    turns = jnp.broadcast_to(row_of(base + 2), full)
+    g_band = tuple(
+        jnp.broadcast_to(packed([gain_band[part, p] for p in range(POLS)]), full)
+        for part in range(2)
+    )
+    turns = jnp.broadcast_to(packed([delay_start[p : p + 1, :] for p in range(POLS)]), full)
 
     def chunk(c):
         return slice(c * width, (c + 1) * width)
@@ -174,6 +208,11 @@
             [(ref[2 * a + b, :, chunk(c)], ref[4 + 2 * a + b, :, chunk(c)]) for b in range(2)]
             for a in range(2)
         ]
+
+    for raw, ref in ((vis_raw, vis), (sky_raw, sky)):
+        for i in range(8):
+            ref[i, :, padded - LANES : padded] = jnp.zeros((times, LANES), jnp.float32)
+            ref[i, :, 0:baselines] = raw[i // 4, i % 4, :, 0, :]
 
     for c in range(chunks):
         v, k = load(vis, c), load(sky, c)
@@ -286,7 +325,7 @@
             s_ref[sweep, c] = power(r[0][0]) + power(r[0][1]) + power(r[1][0]) + power(r[1][1])
             kept.append((gp, gq))
         if sweep == 0:
-            pl.semaphore_wait(barrier, n_freq - 1 + n_tm - 1)
+            pl.semaphore_wait(barrier, n_freq * n_tm - 1)
 
         def scatter_copy(step):
             peer = lax.rem(f_me + step, n_freq)
@@ -396,9 +435,8 @@
         a, e = normal(g, lambda c: w_ref[sweep, c])
         n = turning * conj_mul(g, a)[1]
         d = turning * turning * power(g) * e
-        tile = stack_rows([over_times(n), over_times(d)], 8)
-        tile = exchange(turn_tm_ref.at[sweep], tile, turn_tm_sem.at[sweep], "tm", n_tm, t_me)
-        total = exchange(turn_ref.at[sweep], tile, turn_sem.at[sweep], "freq", n_freq, f_me)
+        tile = stack_rows([over_times(n), over_times(d)], 2)
+        total = exchange_all(turn_ref.at[sweep], tile, turn_sem.at[sweep])
         turns = turns + jnp.broadcast_to(DAMPING * total[0:1] / total[1:2], full)
 
     g, band_delay, phasor = chain()
@@ -423,6 +461,19 @@
     out_params[...] = stack_rows(rows_out, out_params.shape[0])
 
 
+def write_kernel(intervals, params, weights, residual, o_time, o_band, o_delay, o_weights, o_residual):
+    ants = LANES // POLS
+    for p in range(POLS):
+        half = slice(p * ants, (p + 1) * ants)
+        for part in range(2):
+            o_time[part, p] = params[part * intervals : (part + 1) * intervals, half]
+            o_band[part, p] = params[2 * intervals + part : 2 * intervals + part + 1, half]
+        o_delay[p : p + 1, :] = params[2 * intervals + 2 : 2 * intervals + 3, half]
+    o_weights[...] = weights[...]
+    for i in range(8):
+        o_residual[i // 4, i % 4, :, 0, :] = residual[i]
+
+
 def ceil_to(value, step):
     return -(-value // step) * step
 
@@ -437,25 +488,15 @@
     chunks = max(c for c in range(1, min(n_freq, tiles) + 1) if tiles % c == 0)
     width = tiles * LANES // chunks
     padded = tiles * LANES
-    margin = ((0, 0), (0, 0), (0, padded - baselines))
     flat = (8, times, baselines)
     count = 2 * intervals + 3
     height = ceil_to(count, 8)
-    params = jnp.concatenate(
-        [
-            gain_time.transpose(0, 2, 1, 3).reshape(2 * intervals, LANES),
-            gain_band.transpose(0, 2, 1, 3).reshape(2, LANES),
-            delay_start.reshape(1, LANES),
-            jnp.zeros((height - count, LANES), jnp.float32),
-        ],
-        axis=0,
-    )
     sizes = (n_freq, n_tm, channels, times, baselines, chunks, width)
     f32 = jnp.float32
     vmem = pl.BlockSpec(memory_space=pltpu.VMEM)
     sems = [
-        pltpu.SemaphoreType.DMA((SWEEPS, 2, count))
-        for count in (n_freq, n_freq, n_freq, n_tm, n_tm, n_freq)
+        pltpu.SemaphoreType.DMA((SWEEPS, 2) + counts)
+        for counts in ((n_freq,), (n_freq,), (n_freq,), (n_tm,), (n_tm, n_freq))
     ]
     solved, weights, residual = pl.pallas_call(
         functools.partial(kernel, sizes),
@@ -464,9 +505,11 @@
             jax.ShapeDtypeStruct((times, baselines), f32),
             jax.ShapeDtypeStruct(flat, f32),
         ),
-        in_specs=[vmem] * 5,
+        in_specs=[vmem] * 7,
         out_specs=(vmem,) * 3,
         scratch_shapes=[
+            pltpu.VMEM((8, times, padded), f32),
+            pltpu.VMEM((8, times, padded), f32),
             pltpu.VMEM((LANES, 2 * padded), jnp.bfloat16),
             pltpu.VMEM((8, times, padded), f32),
             pltpu.VMEM((4, times, padded), f32),
@@ -477,23 +520,28 @@
             pltpu.VMEM((SWEEPS, chunks, times, width), f32),
             pltpu.VMEM((SWEEPS, n_freq, ceil_to(3 * intervals, 8), LANES), f32),
             pltpu.VMEM((SWEEPS, n_tm, 8, LANES), f32),
-            pltpu.VMEM((SWEEPS, n_tm, 8, LANES), f32),
-            pltpu.VMEM((SWEEPS, n_freq, 8, LANES), f32),
+            pltpu.VMEM((SWEEPS, n_tm, n_freq, 2, LANES), f32),
             *sems,
         ],
         compiler_params=pltpu.CompilerParams(collective_id=0, has_side_effects=True),
     )(
-        jnp.pad(vis.reshape(flat), margin),
-        jnp.pad(sky.reshape(flat), margin),
-        params,
+        vis,
+        sky,
+        gain_time,
+        gain_band,
+        delay_start,
         first.reshape(1, baselines),
         second.reshape(1, baselines),
     )
-    base = 2 * intervals
-    solved_time = solved[0:base].reshape(2, intervals, POLS, antennas).transpose(0, 2, 1, 3)
-    solved_band = solved[base : base + 2].reshape(2, 1, POLS, antennas).transpose(0, 2, 1, 3)
-    solved_delay = solved[base + 2].reshape(POLS, antennas)
-    return solved_time, solved_band, solved_delay, weights, residual.reshape(vis.shape)
+    return pl.pallas_call(
+        functools.partial(write_kernel, intervals),
+        out_shape=tuple(
+            jax.ShapeDtypeStruct(like.shape, f32)
+            for like in (gain_time, gain_band, delay_start, weights, vis)
+        ),
+        in_specs=[vmem] * 3,
+        out_specs=(vmem,) * 5,
+    )(solved, weights, residual)
 
 
 def solution(mesh):

time: 73 us -> 60.9 us (0.83)
  local copies, waits for them, and re-layouts: 10.1 us -> 0 us
  other arithmetic: 1.34 us -> 0 us
    unnamed x17 -> x0, local copies, waits for them, and re-layouts: 6.08 us -> none
    pallas_call x1, Pallas kernels: 60.5 us -> 58.1 us  [shards(): pl.pallas_call(functools.partial(kernel, sizes), out_shape=(jax.ShapeDtyp...]
    pallas_call x0 -> x1, Pallas kernels: none -> 1.97 us  [shards(): pl.pallas_call(functools.partial(write_kernel, intervals), out_shape=tupl...]
    pad x2 -> x0, local copies, waits for them, and re-layouts: 1.65 us -> none  [the longest x1 0.83 us: shards(): jnp.pad(vis.reshape(flat), margin)]
    another operation x3 -> x0, local copies, waits for them, and re-layouts: 1.39 us -> none  [the longest x1 0.66 us: shards(): solved[base:base + 2].reshape(2, 1, POLS, antennas).transpose(0, 2, 1, 3)]
    reshape x4 -> x0, local copies, waits for them, and re-layouts: 0.85 us -> none  [the longest x2 0.68 us: shards(): solved[0:base].reshape(2, intervals, POLS, antennas).transpose(0, 2, 1, 3)]
where the time goes in v1:
time: 60.9 us; the launch traced here: 60.7 us
  Pallas kernels  60 us (99%)
  between operations  0.64 us (1%)
    pallas_call x1, Pallas kernels, shards(): pl.pallas_call(functools.partial(kernel, sizes), out_shape=(jax.ShapeDtyp...  58.1 us
    pallas_call x1, Pallas kernels, shards(): pl.pallas_call(functools.partial(write_kernel, intervals), out_shape=tupl...  1.97 us

profile of v1, /device:TPU:0, one launch (start us, length us, event | category | flops | bytes accessed | tf_op | source)
XLA Modules:
  0.0 60.7 jit_solution(2441540953608885965)
XLA Ops:
  0.6 58.1 %shard_map.110 = (f32[8,128]{1,0:T(8,128)}, f32[8,2016]{1,0:T(8,128)}, f32[8,8,2016]{2,1,0:T(8,128)}) custom-call(f32[2,4,8,1,2016]{4,3,2,1,0:T(1,128)} %vis_raw.1, f32[2,4,8,1,2016]{4,3,2,1,0:T(1,128)} %sky_raw.1, f32[2,2,2,64]{3,2,1,0:T(2,128)} %gain_time.1, f32[2,2,1,64]{3,2,1,0:T(1,128)} %gain_band.1, f32[2,64]{1,0:T(2,128)} %delay_start.1, ...), custom_call_target="tpu_custom_call" | custom-call | tf_op jit(solution)/shard_map/pallas_call | solution.py:501
  58.7 2.0 %shard_map.111 = (f32[2,2,2,64]{3,2,1,0:T(2,128)}, f32[2,2,1,64]{3,2,1,0:T(1,128)}, f32[2,64]{1,0:T(2,128)}, f32[8,2016]{1,0:T(8,128)}, f32[2,4,8,1,2016]{4,3,2,1,0:T(1,128)}) custom-call(f32[8,128]{1,0:T(8,128)} %get-tuple-element.8.params, f32[8,2016]{1,0:T(8,128)} %get-tuple-element.9.weights, f32[8,8,2016]{2,1,0:T(8,128)} %get-tuple-element.10.residual), custom_call_target="tpu_custom_call" | custom-call | tf_op jit(solution)/shard_map/pallas_call | solution.py:536

commit v2 on v1

--- a/solution.py
+++ b/solution.py
@@ -70,7 +70,8 @@
     hot,
     u_ref,
     q_ref,
-    wide,
+    c_ref,
+    g_ref,
     terms,
     s_ref,
     rs_ref,
@@ -260,50 +261,87 @@
                 result[a][b] = (v[a][b][0] - m[0], v[a][b][1] - m[1])
         return result
 
-    def products(c, gp, gq):
-        u = load(u_ref, c)
-        q = [[q_ref[2 * a + b, :, chunk(c)] for b in range(2)] for a in range(2)]
-        pp, pq = [power(x) for x in gp], [power(x) for x in gq]
-        lead = [[None] * 2, [None] * 2]
-        trail = [[None] * 2, [None] * 2]
-        for i in range(2):
-            x, y = cmul(u[i][0], gq[0]), cmul(u[i][1], gq[1])
-            lead[0][i], lead[1][i] = x[0] + y[0], x[1] + y[1]
-            x, y = conj_mul(u[0][i], gp[0]), conj_mul(u[1][i], gp[1])
-            trail[0][i], trail[1][i] = x[0] + y[0], x[1] + y[1]
-        lead_power = [q[i][0] * pq[0] + q[i][1] * pq[1] for i in range(2)]
-        trail_power = [q[0][i] * pp[0] + q[1][i] * pp[1] for i in range(2)]
-        return lead[0] + lead[1] + lead_power, trail[0] + trail[1] + trail_power
-
-    def put_terms(c, tiles, offset, weight):
-        stacked = jnp.concatenate([weight * tile for tile in tiles], axis=0)
-        size = 6 * times
-        for i, part in enumerate(split3(stacked)):
-            terms[i * size : (i + 1) * size, offset + c * width : offset + (c + 1) * width] = part
-
-    def antenna_sums():
+    own_mask = (lane // ants) == lax.rem(row // 2, 2)
+    other_mask = (lane // ants) == lax.rem(row, 2)
+    wide_row = lax.rem(lax.broadcasted_iota(jnp.int32, (times, width), 0), INTERVAL_TIMES)
+
+    def fold(v):
+        even = lax.rem(wide_row, 2) == 0
+        pair = [
+            jnp.where(
+                even,
+                v[k] + pltpu.roll(v[k], times - 1, 0),
+                v[k + 1] + pltpu.roll(v[k + 1], 1, 0),
+            )
+            for k in (0, 2)
+        ]
+        return jnp.where(
+            wide_row < 2,
+            pair[0] + pltpu.roll(pair[0], times - 2, 0),
+            pair[1] + pltpu.roll(pair[1], 2, 0),
+        )
+
+    def swap(x):
+        return jnp.where(
+            wide_row == 1,
+            pltpu.roll(x, times - 1, 0),
+            jnp.where(wide_row == 2, pltpu.roll(x, 1, 0), x),
+        )
+
+    def put_matrices(c, weight):
+        lead = slice(c * width, (c + 1) * width)
+        trail = slice(padded + c * width, padded + (c + 1) * width)
+        folded = [
+            fold([weight * source[base + k, :, lead] for k in range(4)])
+            for source, base in ((u_ref, 0), (u_ref, 4), (q_ref, 0))
+        ]
+        for i, value in enumerate(folded):
+            c_ref[i, :, lead] = value
+            turned = swap(value)
+            c_ref[i, :, trail] = -turned if i == 1 else turned
+
+    def gather_others(g):
+        zero = jnp.zeros(full, jnp.float32)
+        rows = jnp.concatenate([jnp.where(other_mask, x, zero) for x in g], axis=0)
+        rows = jnp.concatenate(split3(rows), axis=0)
+        size = 2 * times
+        for k in range(2 * chunks):
+            source = ((k + chunks) % (2 * chunks)) * width
+            got = jnp.dot(
+                rows, hot[:, source : source + width], preferred_element_type=jnp.float32
+            )
+            got = got[0:size] + got[size : 2 * size] + got[2 * size : 3 * size]
+            g_ref[0, :, k * width : (k + 1) * width] = got[:times]
+            g_ref[1, :, k * width : (k + 1) * width] = got[times:]
+
+    def normal(g):
+        for k in range(2 * chunks):
+            here = slice(k * width, (k + 1) * width)
+            m = (c_ref[0, :, here], c_ref[1, :, here])
+            y = (g_ref[0, :, here], g_ref[1, :, here])
+            x = cmul(m, y)
+            parts = [[], [], []]
+            for tile in (x[0], x[1], c_ref[2, :, here] * power(y)):
+                high = tile.astype(jnp.bfloat16).astype(jnp.float32)
+                rest = tile - high
+                middle = rest.astype(jnp.bfloat16).astype(jnp.float32)
+                for part, value in zip(parts, (high, middle, rest - middle)):
+                    part.append(value)
+            filler = [jnp.zeros((times, width), jnp.float32)]
+            stacked = jnp.concatenate(parts[0] + parts[1] + parts[2] + filler, axis=0)
+            terms[:, here] = stacked.astype(jnp.bfloat16)
         got = lax.dot_general(
             terms[...],
             hot[...],
             (((1,), (1,)), ((), ())),
             preferred_element_type=jnp.float32,
         )
-        size = 6 * times
+        size = 3 * times
         got = got[0:size] + got[size : 2 * size] + got[2 * size : 3 * size]
-        part = [got[i * times : (i + 1) * times] for i in range(6)]
-        return [jnp.where(lower, part[2 * i], part[2 * i + 1]) for i in range(3)]
-
-    def normal(g, weights_at):
-        rows = antenna_rows(g)
-        for c in range(chunks):
-            gp, gq = both(rows, c)
-            lead, trail = products(c, gp, gq)
-            put_terms(c, lead, 0, weights_at(c))
-            put_terms(c, trail, padded, weights_at(c))
-        return finish_normal(g)
-
-    def finish_normal(g):
-        real, imag, e = antenna_sums()
+        zero = jnp.zeros(full, jnp.float32)
+        real, imag, e = [
+            jnp.where(own_mask, got[i * times : (i + 1) * times], zero) for i in range(3)
+        ]
         return (real - g[0] * e, imag - g[1] * e), e
 
     def over_times(x):
@@ -318,12 +356,10 @@
     for sweep in range(SWEEPS):
         g, band_delay, phasor = chain()
         rows = antenna_rows(g)
-        kept = []
         for c in range(chunks):
             gp, gq = both(rows, c)
             r = residual_of(c, gp, gq)
             s_ref[sweep, c] = power(r[0][0]) + power(r[0][1]) + power(r[1][0]) + power(r[1][1])
-            kept.append((gp, gq))
         if sweep == 0:
             pl.semaphore_wait(barrier, n_freq * n_tm - 1)
 
@@ -345,11 +381,7 @@
 
         each_peer(n_freq, send_part)
 
-        for c in range(chunks):
-            gp, gq = kept[c]
-            lead, trail = products(c, gp, gq)
-            for i, tile in enumerate(lead + trail):
-                wide[i, :, chunk(c)] = tile
+        gather_others(g)
 
         def own_copy(step):
             return remote(
@@ -395,10 +427,8 @@
         each_peer(n_freq, sent)
 
         for c in range(chunks):
-            tiles = [wide[i, :, chunk(c)] for i in range(12)]
-            put_terms(c, tiles[:6], 0, w_ref[sweep, c])
-            put_terms(c, tiles[6:], padded, w_ref[sweep, c])
-        a, e = finish_normal(g)
+            put_matrices(c, w_ref[sweep, c])
+        a, e = normal(g)
         n = conj_mul(band_delay, a)
         d = power(band_delay) * e
         rows_out = []
@@ -421,7 +451,8 @@
         )
 
         g, band_delay, phasor = chain()
-        a, e = normal(g, lambda c: w_ref[sweep, c])
+        gather_others(g)
+        a, e = normal(g)
         other = cmul(g_time, phasor)
         n = conj_mul(other, a)
         tile = stack_rows([over_times(x) for x in (n[0], n[1], power(other) * e)], 8)
@@ -432,7 +463,8 @@
         )
 
         g, band_delay, phasor = chain()
-        a, e = normal(g, lambda c: w_ref[sweep, c])
+        gather_others(g)
+        a, e = normal(g)
         n = turning * conj_mul(g, a)[1]
         d = turning * turning * power(g) * e
         tile = stack_rows([over_times(n), over_times(d)], 2)
@@ -483,6 +515,7 @@
     antennas = gain_time.shape[-1]
     assert local_channels == 1 and POLS * antennas == LANES
     intervals = times // INTERVAL_TIMES
+    assert times == 8 and INTERVAL_TIMES == POLS * POLS
     channels = local_channels * n_freq
     tiles = -(-baselines // LANES)
     chunks = max(c for c in range(1, min(n_freq, tiles) + 1) if tiles % c == 0)
@@ -513,8 +546,9 @@
             pltpu.VMEM((LANES, 2 * padded), jnp.bfloat16),
             pltpu.VMEM((8, times, padded), f32),
             pltpu.VMEM((4, times, padded), f32),
-            pltpu.VMEM((12, times, padded), f32),
-            pltpu.VMEM((18 * times, 2 * padded), jnp.bfloat16),
+            pltpu.VMEM((3, times, 2 * padded), f32),
+            pltpu.VMEM((2, times, 2 * padded), f32),
+            pltpu.VMEM((10 * times, 2 * padded), jnp.bfloat16),
             pltpu.VMEM((SWEEPS, chunks, times, width), f32),
             pltpu.VMEM((SWEEPS, n_freq, times, width), f32),
             pltpu.VMEM((SWEEPS, chunks, times, width), f32),

time: 60.9 us -> 59.8 us (0.982)
  Pallas kernels: 60 us -> 59 us
    pallas_call x1, Pallas kernels: 58.1 us -> 57.1 us  [shards(): pl.pallas_call(functools.partial(kernel, sizes), out_shape=(jax.ShapeDtyp...]
where the time goes in v2:
time: 59.8 us; the launch traced here: 59.7 us
  Pallas kernels  59 us (99%)
  between operations  0.64 us (1%)
    pallas_call x1, Pallas kernels, shards(): pl.pallas_call(functools.partial(kernel, sizes), out_shape=(jax.ShapeDtyp...  57.1 us
    pallas_call x1, Pallas kernels, shards(): pl.pallas_call(functools.partial(write_kernel, intervals), out_shape=tupl...  1.97 us

profile of v2, /device:TPU:0, one launch (start us, length us, event | category | flops | bytes accessed | tf_op | source)
XLA Modules:
  0.0 59.7 jit_solution(10372663296390899987)
XLA Ops:
  0.6 57.1 %shard_map.110 = (f32[8,128]{1,0:T(8,128)}, f32[8,2016]{1,0:T(8,128)}, f32[8,8,2016]{2,1,0:T(8,128)}) custom-call(f32[2,4,8,1,2016]{4,3,2,1,0:T(1,128)} %vis_raw.1, f32[2,4,8,1,2016]{4,3,2,1,0:T(1,128)} %sky_raw.1, f32[2,2,2,64]{3,2,1,0:T(2,128)} %gain_time.1, f32[2,2,1,64]{3,2,1,0:T(1,128)} %gain_band.1, f32[2,64]{1,0:T(2,128)} %delay_start.1, ...), custom_call_target="tpu_custom_call" | custom-call | tf_op jit(solution)/shard_map/pallas_call | solution.py:534
  57.7 2.0 %shard_map.111 = (f32[2,2,2,64]{3,2,1,0:T(2,128)}, f32[2,2,1,64]{3,2,1,0:T(1,128)}, f32[2,64]{1,0:T(2,128)}, f32[8,2016]{1,0:T(8,128)}, f32[2,4,8,1,2016]{4,3,2,1,0:T(1,128)}) custom-call(f32[8,128]{1,0:T(8,128)} %get-tuple-element.8.params, f32[8,2016]{1,0:T(8,128)} %get-tuple-element.9.weights, f32[8,8,2016]{2,1,0:T(8,128)} %get-tuple-element.10.residual), custom_call_target="tpu_custom_call" | custom-call | tf_op jit(solution)/shard_map/pallas_call | solution.py:570

commit v3 on v2

--- a/solution.py
+++ b/solution.py
@@ -55,8 +55,8 @@
 
 def kernel(
     sizes,
-    vis_raw,
-    sky_raw,
+    vis_arg,
+    sky_arg,
     gain_time,
     gain_band,
     delay_start,
@@ -65,6 +65,9 @@
     out_params,
     out_weights,
     out_residual,
+    vis_raw,
+    sky_raw,
+    raw_sem,
     vis,
     sky,
     hot,
@@ -112,6 +115,12 @@
         )
 
     each_other(greet)
+    fetches = [
+        pltpu.make_async_copy(source, target, raw_sem.at[i])
+        for i, (source, target) in enumerate(((vis_arg, vis_raw), (sky_arg, sky_raw)))
+    ]
+    for fetch in fetches:
+        fetch.start()
 
     def remote(src, dst, sem, step, axis, count, me):
         return pltpu.make_async_remote_copy(
@@ -154,9 +163,9 @@
         each_other(lambda across, step: copy(across, step).wait_send())
         return total
 
-    row_ant = lax.rem(lax.broadcasted_iota(jnp.int32, (LANES, baselines), 0), ants)
-    hot[:, padded - LANES : padded] = jnp.zeros((LANES, LANES), jnp.bfloat16)
-    hot[:, 2 * padded - LANES : 2 * padded] = jnp.zeros((LANES, LANES), jnp.bfloat16)
+    row_ant = lax.broadcasted_iota(jnp.int32, (ants, baselines), 0)
+    hot[:, padded - LANES : padded] = jnp.zeros((ants, LANES), jnp.bfloat16)
+    hot[:, 2 * padded - LANES : 2 * padded] = jnp.zeros((ants, LANES), jnp.bfloat16)
     hot[:, 0:baselines] = (row_ant == first[...]).astype(jnp.float32).astype(jnp.bfloat16)
     hot[:, padded : padded + baselines] = (
         (row_ant == second[...]).astype(jnp.float32).astype(jnp.bfloat16)
@@ -164,7 +173,6 @@
 
     lane = lax.broadcasted_iota(jnp.int32, (times, LANES), 1)
     row = lax.broadcasted_iota(jnp.int32, (times, LANES), 0)
-    lower = lane < ants
     number = jnp.broadcast_to(f_me, (times, LANES)).astype(jnp.float32)
     frequency = (number + 0.5) / channels - 0.5
     turning = FULL_TURN * frequency
@@ -210,7 +218,8 @@
             for a in range(2)
         ]
 
-    for raw, ref in ((vis_raw, vis), (sky_raw, sky)):
+    for fetch, raw, ref in zip(fetches, (vis_raw, sky_raw), (vis, sky)):
+        fetch.wait()
         for i in range(8):
             ref[i, :, padded - LANES : padded] = jnp.zeros((times, LANES), jnp.float32)
             ref[i, :, 0:baselines] = raw[i // 4, i % 4, :, 0, :]
@@ -231,11 +240,10 @@
         return cmul(g_time, band_delay), band_delay, phasor
 
     def antenna_rows(g):
-        zero = jnp.zeros(full, jnp.float32)
         rows = []
         for part in range(2):
-            rows.append(jnp.where(lower, g[part], zero))
-            rows.append(jnp.where(lower, zero, g[part]))
+            rows.append(g[part][:, :ants])
+            rows.append(g[part][:, ants:])
         return jnp.concatenate(split3(jnp.concatenate(rows, axis=0)), axis=0)
 
     def gathered(rows, c, offset):
@@ -303,6 +311,7 @@
     def gather_others(g):
         zero = jnp.zeros(full, jnp.float32)
         rows = jnp.concatenate([jnp.where(other_mask, x, zero) for x in g], axis=0)
+        rows = rows[:, :ants] + rows[:, ants:]
         rows = jnp.concatenate(split3(rows), axis=0)
         size = 2 * times
         for k in range(2 * chunks):
@@ -338,6 +347,7 @@
         )
         size = 3 * times
         got = got[0:size] + got[size : 2 * size] + got[2 * size : 3 * size]
+        got = jnp.concatenate([got, got], axis=1)
         zero = jnp.zeros(full, jnp.float32)
         real, imag, e = [
             jnp.where(own_mask, got[i * times : (i + 1) * times], zero) for i in range(3)
@@ -538,12 +548,15 @@
             jax.ShapeDtypeStruct((times, baselines), f32),
             jax.ShapeDtypeStruct(flat, f32),
         ),
-        in_specs=[vmem] * 7,
+        in_specs=[pl.BlockSpec(memory_space=pl.ANY)] * 2 + [vmem] * 5,
         out_specs=(vmem,) * 3,
         scratch_shapes=[
+            pltpu.VMEM(vis.shape, f32),
+            pltpu.VMEM(sky.shape, f32),
+            pltpu.SemaphoreType.DMA((2,)),
             pltpu.VMEM((8, times, padded), f32),
             pltpu.VMEM((8, times, padded), f32),
-            pltpu.VMEM((LANES, 2 * padded), jnp.bfloat16),
+            pltpu.VMEM((antennas, 2 * padded), jnp.bfloat16),
             pltpu.VMEM((8, times, padded), f32),
             pltpu.VMEM((4, times, padded), f32),
             pltpu.VMEM((3, times, 2 * padded), f32),

time: 59.8 us -> 59.2 us (0.990)
  Pallas kernels: 59 us -> 58.4 us
    pallas_call x1, Pallas kernels: 57.1 us -> 56.4 us  [shards(): pl.pallas_call(functools.partial(kernel, sizes), out_shape=(jax.ShapeDtyp...]
where the time goes in v3:
time: 59.2 us; the launch traced here: 59 us
  Pallas kernels  58.4 us (99%)
  between operations  0.64 us (1%)
    pallas_call x1, Pallas kernels, shards(): pl.pallas_call(functools.partial(kernel, sizes), out_shape=(jax.ShapeDtyp...  56.4 us
    pallas_call x1, Pallas kernels, shards(): pl.pallas_call(functools.partial(write_kernel, intervals), out_shape=tupl...  1.97 us

profile of v3, /device:TPU:0, one launch (start us, length us, event | category | flops | bytes accessed | tf_op | source)
XLA Modules:
  0.0 59.0 jit_solution(16182232002907506363)
XLA Ops:
  0.6 56.4 %shard_map.110 = (f32[8,128]{1,0:T(8,128)}, f32[8,2016]{1,0:T(8,128)}, f32[8,8,2016]{2,1,0:T(8,128)}) custom-call(f32[2,4,8,1,2016]{4,3,2,1,0:T(1,128)} %vis_arg.1, f32[2,4,8,1,2016]{4,3,2,1,0:T(1,128)} %sky_arg.1, f32[2,2,2,64]{3,2,1,0:T(2,128)} %gain_time.1, f32[2,2,1,64]{3,2,1,0:T(1,128)} %gain_band.1, f32[2,64]{1,0:T(2,128)} %delay_start.1, ...), custom_call_target="tpu_custom_call" | custom-call | tf_op jit(solution)/shard_map/pallas_call | solution.py:544
  57.0 2.0 %shard_map.111 = (f32[2,2,2,64]{3,2,1,0:T(2,128)}, f32[2,2,1,64]{3,2,1,0:T(1,128)}, f32[2,64]{1,0:T(2,128)}, f32[8,2016]{1,0:T(8,128)}, f32[2,4,8,1,2016]{4,3,2,1,0:T(1,128)}) custom-call(f32[8,128]{1,0:T(8,128)} %get-tuple-element.8.params, f32[8,2016]{1,0:T(8,128)} %get-tuple-element.9.weights, f32[8,8,2016]{2,1,0:T(8,128)} %get-tuple-element.10.residual), custom_call_target="tpu_custom_call" | custom-call | tf_op jit(solution)/shard_map/pallas_call | solution.py:583
